TPU v7x, 768 devices: a whole 4x8x12 slice. The times are simulated.
768 devices in a mesh: mesh: 24 (over x, z_lo), harm: 32 (over y, z_hi, core).
Axes of the slice: x: 4, y: 8, z: 12 (z_hi: 2, z_lo: 6; z = z_hi * 6 + z_lo), core: 2. Of those that a mesh axis runs over, the one named last changes fastest.
Arguments:
- current_pattern: float32 [768, 4096], P('mesh'), may hold values from -6 to 6
- conductivity: float32 [768, 4096], P('mesh'), may hold values from 0.5 to 8
- cooling: float32 [768, 4096], P('mesh'), may hold values from 0.05 to 0.5
- harm_order: int32 [32], P('harm'), may hold values from 8 to 64
- harm_amp: int32 [32], P('harm'), may hold values from 1 to 4
- block_counts: int32 [32], P('harm'), may hold values from 1 to 32, as said below
Outputs:
- averaged_dissipation: float32 [768, 4096], P('mesh', 'harm')
- thermal_increase: float32 [768, 4096], P('mesh', 'harm')
Inputs may be any that keep to these rules, and one draw needn't show every extreme that they name: `block_counts`: some harmonic has block count 32.
All inputs are finite; a program needn't handle non-finite values.
Results may differ from a plain program's by a relative error of at most 0.00002.
Values sent between devices are 32-bit elements; how exact they have to be, the bound alone decides.
A program may use at most 32 MiB of HBM per device.

v0:
```python
import jax
import jax.numpy as jnp
from jax import lax
from jax.sharding import PartitionSpec as P

BLK = 128
EDDY_SWEEPS = 3
HEAT_SWEEPS = 4


base_freq = 0.1


def padded(value, sides, width):
    for axis, dim in sides:
        size, length = (lax.axis_size(axis), value.shape[dim])
        up = [(i, (i + 1) % size) for i in range(size - 1)]
        down = [(j, i) for i, j in up]
        last = lax.slice_in_dim(value, length - width, length, axis=dim)
        initial = lax.slice_in_dim(value, 0, width, axis=dim)
        before = lax.ppermute(last, axis, up)
        after = lax.ppermute(initial, axis, down)
        value = jnp.concatenate([before, value, after], axis=dim)
    return value


def bordered_lateral_margin(field):
    widths = [(0, 0)] * (field.ndim - 1) + [(1, 1)]
    return jnp.pad(field, widths)


def eddy_loss(cols, current_pattern, conductivity, omega, amp, count):
    columns = jnp.arange(cols)
    mask = (columns < count * BLK).astype(jnp.float32)[None, :]
    source = amp * current_pattern * mask
    product = omega * conductivity
    denom = 16.0 + product * product
    inv_re = 4.0 / denom
    inv_im = -product / denom
    potential = jnp.stack([source * inv_re, source * inv_im])
    for sweep in range(EDDY_SWEEPS - 1):
        extended_subdomain = padded(potential, (("mesh", 1),), 1)
        outer_margins = bordered_lateral_margin(potential)
        nearby_nodes = (
            extended_subdomain[:, 2:, :]
            + extended_subdomain[:, :-2, :]
            + outer_margins[:, :, 2:]
            + outer_margins[:, :, :-2]
        )
        near_re = source + nearby_nodes[0]
        near_im = nearby_nodes[1]
        potential = jnp.stack(
            [
                mask * (near_re * inv_re - near_im * inv_im),
                mask * (near_re * inv_im + near_im * inv_re),
            ]
        )
    loss = (
        0.5
        * omega
        * omega
        * conductivity
        * (potential[0] * potential[0] + potential[1] * potential[1])
    )
    return loss


def on_device(current_pattern, conductivity, cooling, harm_order, harm_amp, block_counts):
    harmonics = lax.axis_size("harm")
    omega = base_freq * harm_order[0].astype(jnp.float32)
    amp = harm_amp[0].astype(jnp.float32)
    count = block_counts[0]
    width = current_pattern.shape[1]
    local_loss = eddy_loss(width, current_pattern, conductivity, omega, amp, count)
    piece_ratio = width // harmonics
    offset_index = lax.axis_index("harm") * piece_ratio
    entire_dissipation_map = lax.psum(local_loss, "harm") / harmonics
    inverted_weight = 1.0 / (4.0 + cooling)
    thermal_increase = entire_dissipation_map * inverted_weight
    for sweep in range(HEAT_SWEEPS - 1):
        extended_subdomain = padded(thermal_increase, (("mesh", 0),), 1)
        outer_margins = bordered_lateral_margin(thermal_increase)
        nearby_nodes = (
            extended_subdomain[2:, :]
            + extended_subdomain[:-2, :]
            + outer_margins[:, 2:]
            + outer_margins[:, :-2]
        )
        thermal_increase = (entire_dissipation_map + nearby_nodes) * inverted_weight
    averaged_dissipation = lax.dynamic_slice_in_dim(
        entire_dissipation_map, offset_index, piece_ratio, 1
    )
    return (
        averaged_dissipation,
        lax.dynamic_slice_in_dim(thermal_increase, offset_index, piece_ratio, 1),
    )


def solution(mesh):
    return jax.shard_map(
        on_device,
        mesh=mesh,
        in_specs=(
            P("mesh", None),
            P("mesh", None),
            P("mesh", None),
            P("harm"),
            P("harm"),
            P("harm"),
        ),
        out_specs=(P("mesh", "harm"), P("mesh", "harm")),
        check_vma=False,
    )
```

profile of v0, /device:TPU:6, one launch (start us, length us, event | category | flops | bytes accessed | tf_op | source)
XLA Modules:
  0.0 527.8 jit_solution(2796052507473426791)
XLA Ops:
  7.2 0.0 all-reduce.7.cloned.1.call-start
  9.2 1.4 multiply_bitcast_fusion.2
  10.6 13.0 %collective-permute-start = (f32[2,1,4096]{2,1,0:T(1,128)S(1)}, f32[2,1,4096]{2,1,0:T(1,128)S(1)}, u32[]{:S(2)}, u32[]{:S(2)}) collective-permute-start(f32[2,1,4096]{2,1,0:T(1,128)S(1)} %get-tuple-element.10), channel_id=1, source_target_pairs={{32,0},{64,32},{96,64},{128,96},{160,128},{192,160},{224,192},{256... | collective-permute-start | bytes 98312 | tf_op jit(solution)/shard_map/ppermute | solution.py:22
  23.6 1.9 collective-permute-start.1
  25.5 0.1 pad_maximum_fusion
  25.6 0.0 copy-start.2
  25.6 0.0 copy-start.3
  25.7 0.0 collective-permute-done
  25.7 9.5 %collective-permute-done.1 = f32[2,1,4096]{2,1,0:T(1,128)S(1)} collective-permute-done((f32[2,1,4096]{2,1,0:T(1,128)S(1)}, f32[2,1,4096]{2,1,0:T(1,128)S(1)}, u32[]{:S(2)}, u32[]{:S(2)}) %collective-permute-start.1) | collective-permute-done | bytes 32800 | tf_op jit(solution)/shard_map/ppermute | solution.py:21
  35.1 0.7 fusion.5
  35.8 0.0 copy-done.2
  35.8 0.0 copy-done.3
  35.8 0.3 multiply_bitcast_fusion
  36.2 1.9 collective-permute-start.2
  38.1 3.9 collective-permute-start.3
  42.1 0.1 pad_maximum_fusion.1
  42.1 0.0 collective-permute-done.2
  42.2 7.5 %collective-permute-done.3 = f32[2,1,4096]{2,1,0:T(1,128)S(1)} collective-permute-done((f32[2,1,4096]{2,1,0:T(1,128)S(1)}, f32[2,1,4096]{2,1,0:T(1,128)S(1)}, u32[]{:S(2)}, u32[]{:S(2)}) %collective-permute-start.3) | collective-permute-done | bytes 32800 | tf_op jit(solution)/shard_map/ppermute | solution.py:21
  49.7 0.7 fusion.2
  50.3 0.0 copy-start
  50.3 1.2 add_multiply_fusion
  51.6 0.0 all-reduce.7.cloned.1.call-update
  51.6 420.7 %all-reduce.7.cloned.1.call-done = f32[32,4096]{1,0:T(8,128)} async-done(((f32[32,4096]{1,0:T(8,128)}), f32[32,4096]{1,0:T(8,128)}) %all-reduce.7.cloned.1.call-update) | async-done | bytes 524304 | tf_op jit(solution)/shard_map/psum | solution.py:77
  472.2 0.0 copy-done
  472.3 0.0 copy-start.1
  472.3 1.2 broadcast_multiply_fusion
  473.5 8.1 %collective-permute-start.4 = (f32[1,4096]{1,0:T(1,128)S(1)}, f32[1,4096]{1,0:T(1,128)S(1)}, u32[]{:S(2)}, u32[]{:S(2)}) collective-permute-start(f32[1,4096]{1,0:T(1,128)S(1)} %get-tuple-element.21), channel_id=1, source_target_pairs={{32,0},{64,32},{96,64},{128,96},{160,128},{192,160},{224,192},{256... | collective-permute-start | bytes 49160 | tf_op jit(solution)/shard_map/ppermute | solution.py:22
  481.6 1.9 collective-permute-start.5
  483.6 0.0 collective-permute-done.4
  483.6 9.4 %collective-permute-done.5 = f32[1,4096]{1,0:T(1,128)S(1)} collective-permute-done((f32[1,4096]{1,0:T(1,128)S(1)}, f32[1,4096]{1,0:T(1,128)S(1)}, u32[]{:S(2)}, u32[]{:S(2)}) %collective-permute-start.5) | collective-permute-done | bytes 16416 | tf_op jit(solution)/shard_map/ppermute | solution.py:21
  493.0 0.0 copy-done.1
  493.0 0.4 fusion.15
  493.4 1.9 collective-permute-start.6
  495.3 3.9 collective-permute-start.7
  499.2 0.0 collective-permute-done.6
  499.2 7.4 %collective-permute-done.7 = f32[1,4096]{1,0:T(1,128)S(1)} collective-permute-done((f32[1,4096]{1,0:T(1,128)S(1)}, f32[1,4096]{1,0:T(1,128)S(1)}, u32[]{:S(2)}, u32[]{:S(2)}) %collective-permute-start.7) | collective-permute-done | bytes 16416 | tf_op jit(solution)/shard_map/ppermute | solution.py:21
  506.6 0.3 fusion.10
  507.0 1.9 collective-permute-start.8
  508.9 3.9 collective-permute-start.9
  512.9 0.3 pad_slice_fusion.9
  513.2 0.0 collective-permute-done.8
  513.2 7.1 %collective-permute-done.9 = f32[1,4096]{1,0:T(1,128)S(1)} collective-permute-done((f32[1,4096]{1,0:T(1,128)S(1)}, f32[1,4096]{1,0:T(1,128)S(1)}, u32[]{:S(2)}, u32[]{:S(2)}) %collective-permute-start.9) | collective-permute-done | bytes 16416 | tf_op jit(solution)/shard_map/ppermute | solution.py:21
  520.3 0.7 dynamic-slice_multiply_fusion
  (6 shorter events, 0.2 us)
Async XLA Ops:
  7.2 465.1 %all-reduce.7.cloned.1.call-start = ((), (), s32[]{:S(2)}) async-start(), calls=%async_computation | async-start | bytes 1048576 | tf_op jit(solution)/shard_map/psum | solution.py:77
  10.6 15.0 %collective-permute-start = (f32[2,1,4096]{2,1,0:T(1,128)S(1)}, f32[2,1,4096]{2,1,0:T(1,128)S(1)}, u32[]{:S(2)}, u32[]{:S(2)}) collective-permute-start(f32[2,1,4096]{2,1,0:T(1,128)S(1)} %get-tuple-element.10), channel_id=1, source_target_pairs={{32,0},{64,32},{96,64},{128,96},{160,128},{192,160},{224,192},{256... | collective-permute-start | bytes 98312 | tf_op jit(solution)/shard_map/ppermute | solution.py:22
  23.6 11.5 %collective-permute-start.1 = (f32[2,1,4096]{2,1,0:T(1,128)S(1)}, f32[2,1,4096]{2,1,0:T(1,128)S(1)}, u32[]{:S(2)}, u32[]{:S(2)}) collective-permute-start(f32[2,1,4096]{2,1,0:T(1,128)S(1)} %get-tuple-element.11), channel_id=1, source_target_pairs={{0,32},{32,64},{64,96},{96,128},{128,160},{160,192},{192,224},{224... | collective-permute-start | bytes 98312 | tf_op jit(solution)/shard_map/ppermute | solution.py:21
  25.6 10.2 %copy-start.2 = (f32[32,4096]{1,0:T(8,128)S(1)}, f32[32,4096]{1,0:T(8,128)}, u32[]{:S(2)}) copy-start(f32[32,4096]{1,0:T(8,128)} %param.6) | copy-start | bytes 1572868
  25.6 10.2 %copy-start.3 = (f32[32,4096]{1,0:T(8,128)S(1)}, f32[32,4096]{1,0:T(8,128)}, u32[]{:S(2)}) copy-start(f32[32,4096]{1,0:T(8,128)} %param.7) | copy-start | bytes 1572868
  36.2 5.9 %collective-permute-start.2 = (f32[2,1,4096]{2,1,0:T(1,128)S(1)}, f32[2,1,4096]{2,1,0:T(1,128)S(1)}, u32[]{:S(2)}, u32[]{:S(2)}) collective-permute-start(f32[2,1,4096]{2,1,0:T(1,128)S(1)} %get-tuple-element.8), channel_id=1, source_target_pairs={{32,0},{64,32},{96,64},{128,96},{160,128},{192,160},{224,192},{256... | collective-permute-start | bytes 98312 | tf_op jit(solution)/shard_map/ppermute | solution.py:22
  38.1 11.5 %collective-permute-start.3 = (f32[2,1,4096]{2,1,0:T(1,128)S(1)}, f32[2,1,4096]{2,1,0:T(1,128)S(1)}, u32[]{:S(2)}, u32[]{:S(2)}) collective-permute-start(f32[2,1,4096]{2,1,0:T(1,128)S(1)} %get-tuple-element.9), channel_id=1, source_target_pairs={{0,32},{32,64},{64,96},{96,128},{128,160},{160,192},{192,224},{224... | collective-permute-start | bytes 98312 | tf_op jit(solution)/shard_map/ppermute | solution.py:21
  50.3 421.9 %copy-start = (f32[32,4096]{1,0:T(8,128)S(1)}, f32[32,4096]{1,0:T(8,128)}, u32[]{:S(2)}) copy-start(f32[32,4096]{1,0:T(8,128)} %param.8) | copy-start | bytes 1572868
  472.3 20.7 %copy-start.1 = (f32[32,4096]{1,0:T(8,128)S(1)}, f32[32,4096]{1,0:T(8,128)}, u32[]{:S(2)}) copy-start(f32[32,4096]{1,0:T(8,128)} %all-reduce.7.cloned.1.call-done) | copy-start | bytes 1572868
  473.5 10.0 %collective-permute-start.4 = (f32[1,4096]{1,0:T(1,128)S(1)}, f32[1,4096]{1,0:T(1,128)S(1)}, u32[]{:S(2)}, u32[]{:S(2)}) collective-permute-start(f32[1,4096]{1,0:T(1,128)S(1)} %get-tuple-element.21), channel_id=1, source_target_pairs={{32,0},{64,32},{96,64},{128,96},{160,128},{192,160},{224,192},{256... | collective-permute-start | bytes 49160 | tf_op jit(solution)/shard_map/ppermute | solution.py:22
  481.6 11.3 %collective-permute-start.5 = (f32[1,4096]{1,0:T(1,128)S(1)}, f32[1,4096]{1,0:T(1,128)S(1)}, u32[]{:S(2)}, u32[]{:S(2)}) collective-permute-start(f32[1,4096]{1,0:T(1,128)S(1)} %get-tuple-element.22), channel_id=1, source_target_pairs={{0,32},{32,64},{64,96},{96,128},{128,160},{160,192},{192,224},{224... | collective-permute-start | bytes 49160 | tf_op jit(solution)/shard_map/ppermute | solution.py:21
  493.4 5.9 %collective-permute-start.6 = (f32[1,4096]{1,0:T(1,128)S(1)}, f32[1,4096]{1,0:T(1,128)S(1)}, u32[]{:S(2)}, u32[]{:S(2)}) collective-permute-start(f32[1,4096]{1,0:T(1,128)S(1)} %get-tuple-element.19), channel_id=1, source_target_pairs={{32,0},{64,32},{96,64},{128,96},{160,128},{192,160},{224,192},{256... | collective-permute-start | bytes 49160 | tf_op jit(solution)/shard_map/ppermute | solution.py:22
  495.3 11.3 %collective-permute-start.7 = (f32[1,4096]{1,0:T(1,128)S(1)}, f32[1,4096]{1,0:T(1,128)S(1)}, u32[]{:S(2)}, u32[]{:S(2)}) collective-permute-start(f32[1,4096]{1,0:T(1,128)S(1)} %get-tuple-element.20), channel_id=1, source_target_pairs={{0,32},{32,64},{64,96},{96,128},{128,160},{160,192},{192,224},{224... | collective-permute-start | bytes 49160 | tf_op jit(solution)/shard_map/ppermute | solution.py:21
  507.0 6.2 %collective-permute-start.8 = (f32[1,4096]{1,0:T(1,128)S(1)}, f32[1,4096]{1,0:T(1,128)S(1)}, u32[]{:S(2)}, u32[]{:S(2)}) collective-permute-start(f32[1,4096]{1,0:T(1,128)S(1)} %get-tuple-element.15), channel_id=1, source_target_pairs={{32,0},{64,32},{96,64},{128,96},{160,128},{192,160},{224,192},{256... | collective-permute-start | bytes 49160 | tf_op jit(solution)/shard_map/ppermute | solution.py:22
  508.9 11.3 %collective-permute-start.9 = (f32[1,4096]{1,0:T(1,128)S(1)}, f32[1,4096]{1,0:T(1,128)S(1)}, u32[]{:S(2)}, u32[]{:S(2)}) collective-permute-start(f32[1,4096]{1,0:T(1,128)S(1)} %get-tuple-element.16), channel_id=1, source_target_pairs={{0,32},{32,64},{64,96},{96,128},{128,160},{160,192},{192,224},{224... | collective-permute-start | bytes 49160 | tf_op jit(solution)/shard_map/ppermute | solution.py:21
Sparse Core Ops, SparseCore 0:
  51.7 420.5 all-reduce.6
where the time goes:
time: 528 us
  waiting for transfers between devices  462 us (88%)
  starting transfers between devices  42.5 us (8%)
  between operations  16.2 us (3%)
  other arithmetic  7.12 us (1%)
    psum x1, waiting for transfers between devices, on_device(): entire_dissipation_map = lax.psum(local_loss, 'harm') / harmonics  421 us
    ppermute x5, waiting for transfers between devices, padded(): before = lax.ppermute(last, axis, up)  40.8 us
    ppermute x5, starting transfers between devices, padded(): after = lax.ppermute(initial, axis, down)  26.9 us
    ppermute x5, starting transfers between devices, padded(): before = lax.ppermute(last, axis, up)  15.6 us
  transfers between devices with their start and end apart: 11, of which 6 were waited for; matrix products, arithmetic and copies ran while one was open for 0% of the time, Pallas kernels for 0%

commit v1 on v0

v1 whole, which is shorter than its diff:
```python
import functools

import jax
import jax.numpy as jnp
from jax import lax
from jax.experimental import pallas as pl
from jax.experimental.pallas import tpu as pltpu
from jax.sharding import PartitionSpec as P

MESH = pl.DeviceIdType.MESH
BASE_FREQ = 0.1
HARMS = 32
SLABS = 24
ROWS = 32
BLK = 128
WIDE = 2 * BLK
PAD = 8
TALL = ROWS + 2 * PAD
NEAR = (0, 1, 7, 2, 6, 3, 5, 4)
FAR = (4, 5, 3, 6, 2, 7, 1, 0)


def place():
    m, h = lax.axis_index("mesh"), lax.axis_index("harm")
    return m, m // 6, ((h // 2) % 2) * 6 + m % 6, h // 4, h % 2


def device(x, z, y, c):
    return (x % 4) * 6 + z % 6, (y % 8) * 4 + (z // 6) * 2 + c % 2


def slot_of(dz, dy, dc):
    return dz * 16 + NEAR.index(dy) * 2 + dc


def kernel(
    current, conductivity, cooling, msg, mean_out, heat_out,
    field, sides, par, cur_b, con_b, inv_r, inv_i, a_r, a_i, b_r, b_i, weight, total, packed, rec, heat,
    load_sem, int_sem, send_sem, recv_sem, edge_send, edge_recv, all_send, all_recv, out_sem,
):
    m, x, z, y, c = place()
    h = lax.axis_index("harm")
    z_lo = z % 6
    low, high = z < 6, z >= 6
    first, last = z_lo == 0, z_lo == 5
    above = ((m + SLABS - 1) % SLABS, h)
    below = ((m + 1) % SLABS, h)
    barrier = pltpu.get_barrier_semaphore()

    loads = []
    own_row = pltpu.make_async_copy(msg, par.at[pl.ds(0, 1)], int_sem)
    left = jnp.maximum(h - 1, 0)
    right = jnp.minimum(h + 1, HARMS - 1)
    for i, source in enumerate((current, conductivity, cooling)):
        for j, (block, target) in enumerate(
            (
                (h, field.at[i, pl.ds(PAD, ROWS), pl.ds(0, BLK)]),
                (left, sides.at[i, 0]),
                (right, sides.at[i, 1]),
            )
        ):
            columns = pl.ds(pl.multiple_of(block * BLK, BLK), BLK)
            loads.append(pltpu.make_async_copy(source.at[:, columns], target, load_sem.at[i, j]))
    for load in loads:
        load.start()

    def greet(who):
        pl.semaphore_signal(barrier, inc=1, device_id=who, device_id_type=MESH)

    around = [(dy, dc) for dy in FAR for dc in (1, 0)]

    @pl.when(low)
    def _():
        for dy, dc in around:
            if dy or dc:
                greet(device(x, z, y + dy, c + dc))
        for dy, dc in around:
            greet(device(x, 11 - z, y + dy, c + dc))

    @pl.when(jnp.logical_not(last))
    def _():
        greet(below)

    @pl.when(first)
    def _():
        greet(above)

    links = jnp.where(first, 0, 1) + jnp.where(last, 1, 0)
    pl.semaphore_wait(barrier, links + jnp.where(low, 15, 16))

    def row_copy(index, dz, dy, dc):
        slot = slot_of(dz, dy, dc)
        to = device(x, 11 - z if dz else z, y + 8 - dy, c + dc)
        return pltpu.make_async_remote_copy(
            msg, par.at[pl.ds(slot, 1)], send_sem.at[index], recv_sem.at[slot], to, MESH
        )

    @pl.when(high)
    def _():
        for index, (dy, dc) in enumerate(around):
            row_copy(index, 1, dy, dc).start()

    @pl.when(low)
    def _():
        own_row.start()
        for index, (dy, dc) in enumerate(around):
            if dy or dc:
                row_copy(index, 0, dy, dc).start()

    for load in loads:
        load.wait()
    half = lax.broadcasted_iota(jnp.int32, (ROWS, BLK), 1) < BLK // 2
    for i in range(3):
        field[i, PAD : PAD + ROWS, BLK:WIDE] = jnp.where(half, sides[i, 1], sides[i, 0])

    to_below = pltpu.make_async_remote_copy(
        field.at[:, pl.ds(ROWS, PAD)], field.at[:, pl.ds(0, PAD)], edge_send.at[0], edge_recv.at[0], below, MESH
    )
    to_above = pltpu.make_async_remote_copy(
        field.at[:, pl.ds(PAD, PAD)], field.at[:, pl.ds(PAD + ROWS, PAD)], edge_send.at[1], edge_recv.at[1], above, MESH
    )

    @pl.when(jnp.logical_not(first))
    def _():
        to_above.start()

    @pl.when(last)
    def _():
        to_below.start()
        to_above.wait_recv()
        to_below.wait_recv()

    @pl.when(first)
    def _():
        to_above.wait_recv()
        to_below.start()
        to_below.wait_recv()
        to_above.start()

    @pl.when(jnp.logical_not(jnp.logical_or(first, last)))
    def _():
        to_above.wait_recv()
        to_below.start()
        to_below.wait_recv()

    for r in range(2, TALL - 2):
        cur_b[r] = jnp.broadcast_to(field[0, r : r + 1, :], (8, WIDE))
        con_b[r] = jnp.broadcast_to(field[1, r : r + 1, :], (8, WIDE))

    ext_lane = lax.broadcasted_iota(jnp.int32, (8, WIDE), 1)
    block = jnp.where(ext_lane < BLK, h, jnp.where(ext_lane < BLK + BLK // 2, h + 1, h - 1)).astype(jnp.float32)
    up_ok = jnp.where(m > 0, 1.0, 0.0)
    down_ok = jnp.where(m < SLABS - 1, 1.0, 0.0)
    all_copy = pltpu.make_async_remote_copy(par, par, all_send, all_recv, device(x, 11 - z, y, c), MESH)

    def neighbours(ref, at, size):
        mid = ref[pl.ds(at, size)]
        return (ref[pl.ds(at - 1, size)] + ref[pl.ds(at + 1, size)]) + (
            pltpu.roll(mid, 1, 2) + pltpu.roll(mid, WIDE - 1, 2)
        )

    def group(g, carry):
        def arrived(i):
            pltpu.make_async_remote_copy(
                msg, par.at[pl.ds(g * 8 + i, 1)], send_sem.at[0], recv_sem.at[g * 8 + i], below, MESH
            ).wait_recv()

        @pl.when(low)
        def _():
            pl.when(g > 0)(lambda: arrived(0))
            pl.when(g == 0)(own_row.wait)
            for i in range(1, 8):
                arrived(i)

            @pl.when(g == 3)
            def _():
                all_copy.start()

        @pl.when(jnp.logical_and(high, g == 0))
        def _():
            all_copy.wait_recv()

        numbers = par[pl.ds(pl.multiple_of(g * 8, 8), 8), :]
        om = jnp.broadcast_to(numbers[:, 0:1], (8, WIDE))
        am = jnp.broadcast_to(numbers[:, 1:2], (8, WIDE))
        ct = jnp.broadcast_to(numbers[:, 2:3], (8, WIDE))
        mask = jnp.where(jnp.logical_and(block >= 0.0, block < ct), 1.0, 0.0)
        scale = (0.5 / HARMS) * (om * om) * (am * am) * mask

        def first_sweep(at, size, ok):
            con, cur = con_b[pl.ds(at, size)], cur_b[pl.ds(at, size)]
            product = om[None] * con
            inverse = 1.0 / (16.0 + product * product)
            masked = inverse * (mask * ok)[None]
            re = 4.0 * masked
            im = -(product * masked)
            inv_r[pl.ds(at, size)] = re
            inv_i[pl.ds(at, size)] = im
            a_r[pl.ds(at, size)] = cur * re
            a_i[pl.ds(at, size)] = cur * im
            weight[pl.ds(at, size)] = (scale[None] * con) * inverse

        first_sweep(2, 3, up_ok)
        first_sweep(5, 3, up_ok)
        lax.fori_loop(0, 8, lambda i, t: (first_sweep(PAD + 4 * i, 4, 1.0), t)[1], 0)
        first_sweep(PAD + ROWS, 3, down_ok)
        first_sweep(PAD + ROWS + 3, 3, down_ok)

        def second_sweep(i, t):
            at, size = 3 + 3 * i, 3
            near_r = cur_b[pl.ds(at, size)] + neighbours(a_r, at, size)
            near_i = neighbours(a_i, at, size)
            re, im = inv_r[pl.ds(at, size)], inv_i[pl.ds(at, size)]
            b_r[pl.ds(at, size)] = near_r * re - near_i * im
            b_i[pl.ds(at, size)] = near_r * im + near_i * re
            return t

        lax.fori_loop(0, 14, second_sweep, 0)

        def third_sweep(i, t):
            at, size = 4 + 4 * i, 4
            near_r = cur_b[pl.ds(at, size)] + neighbours(b_r, at, size)
            near_i = neighbours(b_i, at, size)
            loss = weight[pl.ds(at, size)] * (near_r * near_r + near_i * near_i)
            total[pl.ds(at, size)] = jnp.where(g == 0, loss, total[pl.ds(at, size)] + loss)
            return t

        lax.fori_loop(0, 10, third_sweep, 0)
        return carry

    def start_total(i, t):
        total[pl.ds(4 + 4 * i, 4)] = jnp.zeros((4, 8, WIDE), jnp.float32)
        return t

    lax.fori_loop(0, 10, start_total, 0)
    lax.fori_loop(0, 4, group, 0)

    packed[...] = jnp.zeros_like(packed)
    for r in range(5, TALL - 5):
        packed[r : r + 1, :] = jnp.sum(total[r], axis=0, keepdims=True)
    row = lax.broadcasted_iota(jnp.int32, (TALL, WIDE), 0)
    col = lax.broadcasted_iota(jnp.int32, (TALL, WIDE), 1)
    inside = jnp.logical_and(
        jnp.logical_and(jnp.logical_or(row >= PAD, m > 0), jnp.logical_or(row < PAD + ROWS, m < SLABS - 1)),
        jnp.logical_and(
            jnp.logical_or(col < BLK + BLK // 2, h > 0),
            jnp.logical_or(jnp.logical_or(col < BLK, col >= BLK + BLK // 2), h < HARMS - 1),
        ),
    )
    share = jnp.where(inside, 1.0 / (4.0 + field[2]), 0.0)
    mean = packed[...]
    warm = mean * share
    for sweep in range(3):
        warm = (
            mean
            + (pltpu.roll(warm, 1, 0) + pltpu.roll(warm, TALL - 1, 0))
            + (pltpu.roll(warm, 1, 1) + pltpu.roll(warm, WIDE - 1, 1))
        ) * share
    heat[...] = warm
    results = [
        pltpu.make_async_copy(source.at[pl.ds(PAD, ROWS), pl.ds(0, BLK)], target, out_sem.at[i])
        for i, (source, target) in enumerate(((packed, mean_out), (heat, heat_out)))
    ]
    for result in results:
        result.start()

    for result in results:
        result.wait()
    to_below.wait_send()
    to_above.wait_send()

    @pl.when(high)
    def _():
        for index, (dy, dc) in enumerate(around):
            row_copy(index, 1, dy, dc).wait_send()

    @pl.when(low)
    def _():
        all_copy.wait_send()
        for index, (dy, dc) in enumerate(around):
            if dy or dc:
                row_copy(index, 0, dy, dc).wait_send()


def on_device(current_pattern, conductivity, cooling, harm_order, harm_amp, block_counts):
    f32 = jnp.float32
    lane = lax.broadcasted_iota(jnp.int32, (1, BLK), 1)
    numbers = (BASE_FREQ * harm_order.astype(f32), harm_amp.astype(f32), block_counts.astype(f32))
    row = jnp.where(lane == 0, numbers[0], jnp.where(lane == 1, numbers[1], numbers[2]))
    tall = pltpu.VMEM((TALL, 8, WIDE), f32)
    return pl.pallas_call(
        kernel,
        out_shape=[jax.ShapeDtypeStruct((ROWS, BLK), f32)] * 2,
        in_specs=[pl.BlockSpec(memory_space=pltpu.HBM)] * 4,
        out_specs=[pl.BlockSpec(memory_space=pltpu.HBM)] * 2,
        scratch_shapes=[
            pltpu.VMEM((3, TALL, WIDE), f32),
            pltpu.VMEM((3, 2, ROWS, BLK), f32),
            pltpu.VMEM((HARMS, BLK), f32),
            tall, tall, tall, tall, tall, tall, tall, tall, tall, tall,
            pltpu.VMEM((TALL, WIDE), f32),
            pltpu.VMEM((TALL, WIDE), f32),
            pltpu.VMEM((TALL, WIDE), f32),
            pltpu.SemaphoreType.DMA((3, 3)),
            pltpu.SemaphoreType.DMA,
            pltpu.SemaphoreType.DMA((16,)),
            pltpu.SemaphoreType.DMA((HARMS,)),
            pltpu.SemaphoreType.DMA((2,)),
            pltpu.SemaphoreType.DMA((2,)),
            pltpu.SemaphoreType.DMA,
            pltpu.SemaphoreType.DMA,
            pltpu.SemaphoreType.DMA((2,)),
        ],
        compiler_params=pltpu.CompilerParams(collective_id=0, has_side_effects=True),
    )(current_pattern, conductivity, cooling, row)


def solution(mesh):
    return jax.shard_map(
        on_device,
        mesh=mesh,
        in_specs=(
            P("mesh", None),
            P("mesh", None),
            P("mesh", None),
            P("harm"),
            P("harm"),
            P("harm"),
        ),
        out_specs=(P("mesh", "harm"), P("mesh", "harm")),
        check_vma=False,
    )
```

time: 528 us -> 47.5 us (0.09)
  the two profiles are of different devices: /device:TPU:6 before, /device:TPU:390 now
where the time goes in v1:
time: 47.5 us; the launch traced here: 47.2 us
  Pallas kernels  42.1 us (89%)
  between operations  2.59 us (5%)
  local copies, waits for them, and re-layouts  1.94 us (4%)
  other arithmetic  0.55 us (1%)
    pallas_call x1, Pallas kernels, on_device(): pl.pallas_call(kernel, out_shape=[jax.ShapeDtypeStruct((ROWS, BLK), f32)]...  42.1 us
    unnamed x4, local copies, waits for them, and re-layouts  1.94 us

profile of v1, /device:TPU:390, one launch (start us, length us, event | category | flops | bytes accessed | tf_op | source)
XLA Modules:
  0.0 47.2 jit_solution(286958575109465641)
XLA Ops:
  2.6 0.5 %compare_select_fusion.1.msg = f32[1,128]{1,0:T(1,128)} fusion(f32[]{:T(128)} %bitcast.2, f32[]{:T(128)} %bitcast.1, f32[]{:T(128)} %bitcast), kind=kLoop, calls=%fused_computation.1 | loop fusion | flops 512 | bytes 524 | tf_op jit(solution)/shard_map/jit(_where)/select_n | solution.py:289
  3.1 42.1 %shard_map.77 = (f32[32,128]{1,0:T(8,128)}, f32[32,128]{1,0:T(8,128)}) custom-call(f32[32,4096]{1,0:T(8,128)} %current.1, f32[32,4096]{1,0:T(8,128)} %conductivity.1, f32[32,4096]{1,0:T(8,128)} %cooling.1, f32[1,128]{1,0:T(1,128)} %compare_select_fusion.1.msg), custom_call_target="tpu_custom_call" | custom-call | tf_op jit(solution)/shard_map/pallas_call | solution.py:291
  45.2 0.0 copy-start
  45.2 1.3 %copy.13 = f32[32,128]{1,0:T(8,128)} copy(f32[32,128]{1,0:T(8,128)} %get-tuple-element.4) | data formatting | bytes 32768
  46.6 0.0 copy-done
  46.6 0.6 %copy.14 = f32[32,128]{1,0:T(8,128)} copy(f32[32,128]{1,0:T(8,128)S(1)} %copy-done) | data formatting | bytes 32768
Async XLA Ops:
  45.2 1.3 %copy-start = (f32[32,128]{1,0:T(8,128)S(1)}, f32[32,128]{1,0:T(8,128)}, u32[]{:S(2)}) copy-start(f32[32,128]{1,0:T(8,128)} %get-tuple-element.5) | copy-start | bytes 49156

commit v2 on v1

v2 whole, which is shorter than its diff:
```python
import functools

import jax
import jax.numpy as jnp
from jax import lax
from jax.experimental import pallas as pl
from jax.experimental.pallas import tpu as pltpu
from jax.sharding import PartitionSpec as P

MESH = pl.DeviceIdType.MESH
BASE_FREQ = 0.1
HARMS = 32
SLABS = 24
ROWS = 32
BLK = 128
WIDE = 2 * BLK
PAD = 8
TALL = ROWS + 2 * PAD
RING = HARMS // 2


def place():
    m, h = lax.axis_index("mesh"), lax.axis_index("harm")
    return m, m // 6, ((h // 2) % 2) * 6 + m % 6, h // 4, h % 2


def device(x, z, y, c):
    return (x % 4) * 6 + z % 6, (y % 8) * 4 + (z // 6) * 2 + c % 2


def offset(i):
    k = i // 2
    return (4 + (k % 2) * ((k + 1) // 2) - (1 - k % 2) * (k // 2)) % 8, 1 - i % 2


def kernel(
    current, conductivity, cooling, order, amp, count, both,
    field, sides, other, other_parts, ints, msg, par, cur_b, con_b, inv_r, inv_i, a_r, a_i, b_r, b_i, weight, total, packed,
    load_sem, other_sem, int_sem, send_sem, recv_sem, edge_send, edge_recv, all_send, all_recv,
):
    m, x, z, y, c = place()
    h = lax.axis_index("harm")
    z_lo = z % 6
    low, high = z < 6, z >= 6
    first, last = z_lo == 0, z_lo == 5
    above = ((m + SLABS - 1) % SLABS, h)
    below = ((m + 1) % SLABS, h)
    barrier = pltpu.get_barrier_semaphore()

    loads = []
    for i, (source, target) in enumerate(zip((order, amp, count), ints)):
        loads.append(pltpu.make_async_copy(source, target, int_sem.at[i]))
    left = jnp.maximum(h - 1, 0)
    right = jnp.minimum(h + 1, HARMS - 1)
    for i, source in enumerate((current, conductivity, cooling)):
        for j, (block, target) in enumerate(
            (
                (h, field.at[i, pl.ds(PAD, ROWS), pl.ds(0, BLK)]),
                (left, sides.at[i, 0]),
                (right, sides.at[i, 1]),
            )
        ):
            columns = pl.ds(pl.multiple_of(block * BLK, BLK), BLK)
            loads.append(pltpu.make_async_copy(source.at[:, columns], target, load_sem.at[i, j]))
    for load in loads:
        load.start()
    lends = jnp.logical_or(z == 6, z == 11)
    lent_rows = pl.ds(pl.multiple_of(jnp.where(z == 6, 0, ROWS - PAD), PAD), PAD)
    other_loads = []
    for i, source in enumerate((current, conductivity, cooling)):
        for j, block in enumerate((h - 2, jnp.maximum(h - 3, 0), h - 1)):
            columns = pl.ds(pl.multiple_of(block * BLK, BLK), BLK)
            other_loads.append(
                pltpu.make_async_copy(source.at[lent_rows, columns], other_parts.at[i, j], other_sem.at[i, j])
            )

    @pl.when(lends)
    def _():
        for load in other_loads:
            load.start()


    def greet(who):
        pl.semaphore_signal(barrier, inc=1, device_id=who, device_id_type=MESH)

    def for_each(count, do):
        def step(i, t):
            do(i)
            return t

        lax.fori_loop(0, count, step, 0)

    @pl.when(jnp.logical_not(last))
    def _():
        greet(below)

    @pl.when(z == 5)
    def _():
        greet(device(x + 1, 6, y, c))

    @pl.when(z == 6)
    def _():
        greet(above)

    @pl.when(z == 0)
    def _():
        greet(device(x + 3, 11, y, c))

    def greet_offset(i, height):
        dy, dc = offset(i)
        greet(device(x, height, y + dy, c + dc))

    @pl.when(low)
    def _():
        for_each(RING - 1, lambda i: greet_offset(i, z))
        for_each(RING, lambda i: greet_offset(i, 11 - z))

    for load in loads[:3]:
        load.wait()
    lane = lax.broadcasted_iota(jnp.int32, (1, BLK), 1)
    omega = BASE_FREQ * jnp.full((1, BLK), ints[0][0], jnp.int32).astype(jnp.float32)
    amps = jnp.full((1, BLK), ints[1][0], jnp.int32).astype(jnp.float32)
    counts = jnp.full((1, BLK), ints[2][0], jnp.int32).astype(jnp.float32)
    msg[...] = jnp.where(lane == 0, omega, jnp.where(lane == 1, amps, counts))

    links = jnp.where(z == 0, 0, 1) + jnp.where(z == 11, 2, 0)
    pl.semaphore_wait(barrier, links + jnp.where(low, 15, 16))

    def row_copy(i, other_half):
        dy, dc = offset(i)
        slot = RING * other_half + RING - 1 - i
        to = device(x, 11 - z if other_half else z, y + 8 - dy, c + dc)
        return pltpu.make_async_remote_copy(
            msg, par.at[pl.ds(slot, 1)], send_sem.at[RING * other_half + i], recv_sem.at[slot], to, MESH
        )

    @pl.when(high)
    def _():
        for_each(RING, lambda i: row_copy(i, 1).start())

    @pl.when(low)
    def _():
        par[0:1, :] = msg[...]
        for_each(RING - 1, lambda i: row_copy(i, 0).start())

    for load in loads[3:]:
        load.wait()
    half = lax.broadcasted_iota(jnp.int32, (ROWS, BLK), 1) < BLK // 2
    for i in range(3):
        field[i, PAD : PAD + ROWS, BLK:WIDE] = jnp.where(half, sides[i, 1], sides[i, 0])

    to_below = pltpu.make_async_remote_copy(
        field.at[:, pl.ds(ROWS, PAD)], field.at[:, pl.ds(0, PAD)], edge_send.at[0], edge_recv.at[0], below, MESH
    )
    to_above = pltpu.make_async_remote_copy(
        field.at[:, pl.ds(PAD, PAD)], field.at[:, pl.ds(PAD + ROWS, PAD)], edge_send.at[1], edge_recv.at[1], above, MESH
    )

    to_fifth = pltpu.make_async_remote_copy(
        other,
        field.at[:, pl.ds(PAD + ROWS, PAD)],
        edge_send.at[2],
        edge_recv.at[1],
        device(x + 3, 5, y, c),
        MESH,
    )

    to_zero = pltpu.make_async_remote_copy(
        other, field.at[:, pl.ds(0, PAD)], edge_send.at[2], edge_recv.at[0], device(x + 1, 0, y, c), MESH
    )

    @pl.when(jnp.logical_not(first))
    def _():
        to_above.start()

    @pl.when(lends)
    def _():
        for load in other_loads:
            load.wait()
        for i in range(3):
            other[i, :, 0:BLK] = other_parts[i, 0]
            other[i, :, BLK:WIDE] = jnp.where(half[0:PAD], other_parts[i, 2], other_parts[i, 1])
        pl.when(z == 6)(to_fifth.start)
        pl.when(z == 11)(to_zero.start)

    @pl.when(z == 11)
    def _():
        to_below.start()

    to_above.wait_recv()

    @pl.when(jnp.logical_not(last))
    def _():
        to_below.start()

    to_below.wait_recv()

    @pl.when(z == 6)
    def _():
        to_above.start()

    for r in range(2, TALL - 2):
        cur_b[r] = jnp.broadcast_to(field[0, r : r + 1, :], (8, WIDE))
        con_b[r] = jnp.broadcast_to(field[1, r : r + 1, :], (8, WIDE))

    ext_lane = lax.broadcasted_iota(jnp.int32, (8, WIDE), 1)
    block = jnp.where(ext_lane < BLK, h, jnp.where(ext_lane < BLK + BLK // 2, h + 1, h - 1)).astype(jnp.float32)
    up_ok = jnp.where(m > 0, 1.0, 0.0)
    down_ok = jnp.where(m < SLABS - 1, 1.0, 0.0)
    all_copy = pltpu.make_async_remote_copy(
        par, par, all_send, all_recv, device(x, 11 - z, y, c), MESH
    )

    def neighbours(ref, at, size):
        mid = ref[pl.ds(at, size)]
        return (ref[pl.ds(at - 1, size)] + ref[pl.ds(at + 1, size)]) + (
            pltpu.roll(mid, 1, 2) + pltpu.roll(mid, WIDE - 1, 2)
        )

    def group(g, carry):
        def arrived(i):
            pltpu.make_async_remote_copy(
                msg, par.at[pl.ds(g * 8 + i, 1)], send_sem.at[0], recv_sem.at[g * 8 + i], below, MESH
            ).wait_recv()

        @pl.when(low)
        def _():
            pl.when(g > 0)(lambda: arrived(0))
            for_each(7, lambda i: arrived(i + 1))

        @pl.when(jnp.logical_and(low, g == 3))
        def _():
            all_copy.start()

        @pl.when(jnp.logical_and(high, g == 0))
        def _():
            all_copy.wait_recv()

        numbers = par[pl.ds(pl.multiple_of(g * 8, 8), 8), :]
        om = jnp.broadcast_to(numbers[:, 0:1], (8, WIDE))
        am = jnp.broadcast_to(numbers[:, 1:2], (8, WIDE))
        ct = jnp.broadcast_to(numbers[:, 2:3], (8, WIDE))
        mask = jnp.where(jnp.logical_and(block >= 0.0, block < ct), 1.0, 0.0)
        scale = 0.5 * (om * om) * (am * am) * mask

        def first_sweep(at, size, ok):
            con, cur = con_b[pl.ds(at, size)], cur_b[pl.ds(at, size)]
            product = om[None] * con
            inverse = 1.0 / (16.0 + product * product)
            masked = inverse * (mask * ok)[None]
            re = 4.0 * masked
            im = -(product * masked)
            inv_r[pl.ds(at, size)] = re
            inv_i[pl.ds(at, size)] = im
            a_r[pl.ds(at, size)] = cur * re
            a_i[pl.ds(at, size)] = cur * im
            weight[pl.ds(at, size)] = (scale[None] * con) * inverse

        first_sweep(2, 3, up_ok)
        first_sweep(5, 3, up_ok)
        lax.fori_loop(0, 8, lambda i, t: (first_sweep(PAD + 4 * i, 4, 1.0), t)[1], 0, unroll=True)
        first_sweep(PAD + ROWS, 3, down_ok)
        first_sweep(PAD + ROWS + 3, 3, down_ok)

        def second_sweep(i, t):
            at, size = 3 + 3 * i, 3
            near_r = cur_b[pl.ds(at, size)] + neighbours(a_r, at, size)
            near_i = neighbours(a_i, at, size)
            re, im = inv_r[pl.ds(at, size)], inv_i[pl.ds(at, size)]
            b_r[pl.ds(at, size)] = near_r * re - near_i * im
            b_i[pl.ds(at, size)] = near_r * im + near_i * re
            return t

        lax.fori_loop(0, 14, second_sweep, 0, unroll=True)

        def third_sweep(i, t):
            at, size = 4 + 4 * i, 4
            near_r = cur_b[pl.ds(at, size)] + neighbours(b_r, at, size)
            near_i = neighbours(b_i, at, size)
            loss = weight[pl.ds(at, size)] * (near_r * near_r + near_i * near_i)
            total[pl.ds(at, size)] = jnp.where(g == 0, loss, total[pl.ds(at, size)] + loss)
            return t

        lax.fori_loop(0, 10, third_sweep, 0, unroll=True)
        return carry

    def start_total(i, t):
        total[pl.ds(4 + 4 * i, 4)] = jnp.zeros((4, 8, WIDE), jnp.float32)
        return t

    lax.fori_loop(0, 10, start_total, 0)
    lax.fori_loop(0, 4, group, 0)

    packed[...] = jnp.zeros_like(packed)
    for r in range(5, TALL - 5):
        packed[r : r + 1, :] = jnp.sum(total[r], axis=0, keepdims=True)
    row = lax.broadcasted_iota(jnp.int32, (TALL, WIDE), 0)
    col = lax.broadcasted_iota(jnp.int32, (TALL, WIDE), 1)
    inside = jnp.logical_and(
        jnp.logical_and(jnp.logical_or(row >= PAD, m > 0), jnp.logical_or(row < PAD + ROWS, m < SLABS - 1)),
        jnp.logical_and(
            jnp.logical_or(col < BLK + BLK // 2, h > 0),
            jnp.logical_or(jnp.logical_or(col < BLK, col >= BLK + BLK // 2), h < HARMS - 1),
        ),
    )
    share = jnp.where(inside, 1.0 / (4.0 + field[2]), 0.0)
    mean = packed[...]
    warm = mean * share
    for sweep in range(3):
        warm = (
            mean
            + (pltpu.roll(warm, 1, 0) + pltpu.roll(warm, TALL - 1, 0))
            + (pltpu.roll(warm, 1, 1) + pltpu.roll(warm, WIDE - 1, 1))
        ) * share
    both[0] = mean[PAD : PAD + ROWS, 0:BLK]
    both[1] = warm[PAD : PAD + ROWS, 0:BLK]

    @pl.when(z != 5)
    def _():
        to_below.wait_send()

    @pl.when(z == 11)
    def _():
        to_zero.wait_send()


    @pl.when(z != 0)
    def _():
        to_above.wait_send()

    @pl.when(z == 6)
    def _():
        to_fifth.wait_send()

    @pl.when(high)
    def _():
        for_each(RING, lambda i: row_copy(i, 1).wait_send())

    @pl.when(low)
    def _():
        all_copy.wait_send()
        for_each(RING - 1, lambda i: row_copy(i, 0).wait_send())


def exchange_and_solve(current_pattern, conductivity, cooling, harm_order, harm_amp, block_counts):
    f32 = jnp.float32
    tall = pltpu.VMEM((TALL, 8, WIDE), f32)
    return pl.pallas_call(
        kernel,
        out_shape=jax.ShapeDtypeStruct((2, ROWS, BLK), f32),
        in_specs=[pl.BlockSpec(memory_space=pltpu.HBM)] * 6,
        out_specs=pl.BlockSpec(memory_space=pltpu.VMEM),
        scratch_shapes=[
            pltpu.VMEM((3, TALL, WIDE), f32),
            pltpu.VMEM((3, 2, ROWS, BLK), f32),
            pltpu.VMEM((3, PAD, WIDE), f32),
            pltpu.VMEM((3, 3, PAD, BLK), f32),
            [pltpu.SMEM((1,), jnp.int32)] * 3,
            pltpu.VMEM((1, BLK), f32),
            pltpu.VMEM((HARMS, BLK), f32),
            tall, tall, tall, tall, tall, tall, tall, tall, tall, tall,
            pltpu.VMEM((TALL, WIDE), f32),
            pltpu.SemaphoreType.DMA((3, 3)),
            pltpu.SemaphoreType.DMA((3, 3)),
            pltpu.SemaphoreType.DMA((3,)),
            pltpu.SemaphoreType.DMA((HARMS,)),
            pltpu.SemaphoreType.DMA((HARMS,)),
            pltpu.SemaphoreType.DMA((3,)),
            pltpu.SemaphoreType.DMA((2,)),
            pltpu.SemaphoreType.DMA,
            pltpu.SemaphoreType.DMA,
        ],
        compiler_params=pltpu.CompilerParams(collective_id=0, has_side_effects=True),
    )(current_pattern, conductivity, cooling, harm_order, harm_amp, block_counts)


def on_device(*args):
    both = lax.cond(
        lax.axis_index("harm") < HARMS,
        exchange_and_solve,
        lambda *a: jnp.zeros((2, ROWS, BLK), jnp.float32),
        *args,
    )
    return both[0] * (1.0 / HARMS), both[1] * (1.0 / HARMS)


def solution(mesh):
    return jax.shard_map(
        on_device,
        mesh=mesh,
        in_specs=(
            P("mesh", None),
            P("mesh", None),
            P("mesh", None),
            P("harm"),
            P("harm"),
            P("harm"),
        ),
        out_specs=(P("mesh", "harm"), P("mesh", "harm")),
        check_vma=False,
    )
```

time: 47.5 us -> 28.7 us (0.60)
  the two profiles are of different devices: /device:TPU:390 before, /device:TPU:1 now
where the time goes in v2:
time: 28.7 us; the launch traced here: 28.5 us
  Pallas kernels  27.2 us (95%)
  between operations  0.64 us (2%)
  other arithmetic  0.62 us (2%)
    pallas_call x1, Pallas kernels, exchange_and_solve(): pl.pallas_call(kernel, out_shape=jax.ShapeDtypeStruct((2, ROWS, BLK), f32...  27.2 us
    mul x1, other arithmetic, on_device(): return (both[0] * (1.0 / HARMS), both[1] * (1.0 / HARMS))  0.62 us

profile of v2, /device:TPU:1, one launch (start us, length us, event | category | flops | bytes accessed | tf_op | source)
XLA Modules:
  0.0 28.5 jit_solution(9631980363799064684)
XLA Ops:
  0.6 27.3 %conditional.1 = (f32[2,32,128]{2,1,0:T(8,128)S(1)}) conditional(s32[]{:T(128)} %convert_element_type.3, () %tuple.14, (f32[32,4096]{1,0:T(8,128)}, f32[32,4096]{1,0:T(8,128)}, f32[32,4096]{1,0:T(8,128)}, s32[1]{0:T(128)}, s32[1]{0:T(128)}, /*index=5*/s32[1]{0:T(128)}) %tuple.15), branch_computations={%region_0.0_spmd, %region_1.0_spmd} | conditional | bytes 32780 | solution.py:378
  0.6 27.2 %branch_1_fun.1 = f32[2,32,128]{2,1,0:T(8,128)S(1)} custom-call(f32[32,4096]{1,0:T(8,128)} %get-tuple-element.29.current, f32[32,4096]{1,0:T(8,128)} %get-tuple-element.30.conductivity, f32[32,4096]{1,0:T(8,128)} %get-tuple-element.31.cooling, s32[1]{0:T(128)} %get-tuple-element.32.order, s32[1]{0:T(128)} %get-tuple-element.33.amp, s32[1]{0:T(128)} %get-tuple-element.34.count), custom_call_target="tpu_custom_call" | custom-call | tf_op jit(solution)/shard_map/cond/branch_1_fun/pallas_call | solution.py:348
  27.9 0.6 %multiply_bitcast_fusion = (f32[32,128]{1,0:T(8,128)}, f32[32,128]{1,0:T(8,128)}) fusion(f32[2,32,128]{2,1,0:T(8,128)S(1)} %get-tuple-element.37), kind=kLoop, calls=%fused_computation | loop fusion | flops 8192 | bytes 65536 | tf_op jit(solution)/shard_map/mul | solution.py:384

commit v3 on v2

v3 whole, which is shorter than its diff:
```python
import functools

import jax
import jax.numpy as jnp
from jax import lax
from jax.experimental import pallas as pl
from jax.experimental.pallas import tpu as pltpu
from jax.sharding import PartitionSpec as P

MESH = pl.DeviceIdType.MESH
BASE_FREQ = 0.1
HARMS = 32
SLABS = 24
ROWS = 32
BLK = 128
WIDE = 2 * BLK
PAD = 8
TALL = ROWS + 2 * PAD
RING = HARMS // 2


AROUND = tuple((dy, dc) for dy in (4, 5, 3, 6, 2, 7, 1, 0) for dc in (1, 0))


def steps_below(value, step, count):
    return sum((value >= step * k).astype(jnp.int32) for k in range(1, count))


def kernel(
    current, conductivity, cooling, order, amp, count, both,
    field, parts, other, other_parts, msg, par, cur_b, con_b, inv_r, inv_i, a_r, a_i, b_r, b_i, weight, total, packed,
    load_sem, other_sem, send_sem, recv_sem, edge_send, edge_recv, all_send, all_recv,
):
    m, h = lax.axis_index("mesh"), lax.axis_index("harm")
    x, y = steps_below(m, 6, 4), steps_below(h, 4, 8)
    z_lo = m - 6 * x
    z_hi = (h - 4 * y >= 2).astype(jnp.int32)
    c = h - 4 * y - 2 * z_hi
    z = z_lo + 6 * z_hi
    low, high = z < 6, z >= 6
    last = z_lo == 5
    above = (jnp.where(m == 0, SLABS - 1, m - 1), h)
    below = (jnp.where(m == SLABS - 1, 0, m + 1), h)
    after = jnp.where(x == 3, m - 18, m + 6) - 5
    before = jnp.where(x == 0, m + 18, m - 6) + 5
    own_half = [2 * z_hi + c, 2 * z_hi + (1 - c)]
    other_half = [2 * (1 - z_hi) + c, 2 * (1 - z_hi) + (1 - c)]
    around_y = [4 * jnp.where(y + d >= 8, y + d - 8, y + d) for d in range(8)]
    mirror = jnp.where(z_lo < 3, m + 3, m - 3)

    def inside(dy, dc):
        return m, around_y[dy % 8] + own_half[dc]

    def across(dy, dc):
        return mirror, around_y[dy % 8] + other_half[dc]

    barrier = pltpu.get_barrier_semaphore()

    left = jnp.maximum(h - 1, 0)
    right = jnp.minimum(h + 1, HARMS - 1)
    for i, source in enumerate((current, conductivity, cooling)):
        for j, block in enumerate((h, left, right)):
            columns = pl.ds(pl.multiple_of(block * BLK, BLK), BLK)
            pltpu.make_async_copy(source.at[:, columns], parts.at[i, j], load_sem).start()
    lends = jnp.logical_or(z == 6, z == 11)
    lent_rows = pl.ds(pl.multiple_of(jnp.where(z == 6, 0, ROWS - PAD), PAD), PAD)

    @pl.when(lends)
    def _():
        for i, source in enumerate((current, conductivity, cooling)):
            for j, block in enumerate((h - 2, jnp.maximum(h - 3, 0), h - 1)):
                columns = pl.ds(pl.multiple_of(block * BLK, BLK), BLK)
                pltpu.make_async_copy(source.at[lent_rows, columns], other_parts.at[i, j], other_sem).start()

    def greet(who):
        pl.semaphore_signal(barrier, inc=1, device_id=who, device_id_type=MESH)

    @pl.when(jnp.logical_not(last))
    def _():
        greet(below)

    @pl.when(z == 5)
    def _():
        greet((after, h + 2))

    @pl.when(z == 6)
    def _():
        greet(above)

    @pl.when(z == 0)
    def _():
        greet((before, h + 2))

    @pl.when(low)
    def _():
        for dy, dc in AROUND[:-1]:
            greet(inside(dy, dc))
        for dy, dc in AROUND:
            greet(across(dy, dc))

    lane = lax.broadcasted_iota(jnp.int32, (1, BLK), 1)
    numbers = [jnp.full((1, BLK), v[0], jnp.int32) for v in (order, amp, count)]
    msg[...] = jnp.where(lane == 0, numbers[0], jnp.where(lane == 1, numbers[1], numbers[2])).astype(jnp.float32)

    links = jnp.where(z == 0, 0, 1) + jnp.where(z == 11, 2, 0)
    pl.semaphore_wait(barrier, links + jnp.where(low, 15, 16))

    def row_copy(i, crossing):
        dy, dc = AROUND[i]
        slot = RING * crossing + RING - 1 - i
        return pltpu.make_async_remote_copy(
            msg,
            par.at[pl.ds(slot, 1)],
            send_sem,
            recv_sem.at[slot // 8],
            (across if crossing else inside)(-dy, dc),
            MESH,
        )

    @pl.when(high)
    def _():
        for i in range(RING):
            row_copy(i, 1).start()

    @pl.when(low)
    def _():
        par[0:1, :] = msg[...]
        for i in range(RING - 1):
            row_copy(i, 0).start()

    pltpu.make_async_copy(parts, parts, load_sem).wait()
    half = lax.broadcasted_iota(jnp.int32, (ROWS, BLK), 1) < BLK // 2
    for i in range(3):
        field[i, PAD : PAD + ROWS, 0:BLK] = parts[i, 0]
        field[i, PAD : PAD + ROWS, BLK:WIDE] = jnp.where(half, parts[i, 2], parts[i, 1])

    to_below = pltpu.make_async_remote_copy(
        field.at[:, pl.ds(ROWS, PAD)], field.at[:, pl.ds(0, PAD)], edge_send.at[0], edge_recv.at[0], below, MESH
    )
    to_above = pltpu.make_async_remote_copy(
        field.at[:, pl.ds(PAD, PAD)], field.at[:, pl.ds(PAD + ROWS, PAD)], edge_send.at[1], edge_recv.at[1], above, MESH
    )

    to_fifth = pltpu.make_async_remote_copy(
        other,
        field.at[:, pl.ds(PAD + ROWS, PAD)],
        edge_send.at[2],
        edge_recv.at[1],
        (before, h - 2),
        MESH,
    )

    to_zero = pltpu.make_async_remote_copy(
        other, field.at[:, pl.ds(0, PAD)], edge_send.at[2], edge_recv.at[0], (after, h - 2), MESH
    )

    @pl.when(z_lo != 0)
    def _():
        to_above.start()

    @pl.when(lends)
    def _():
        pltpu.make_async_copy(other_parts, other_parts, other_sem).wait()
        for i in range(3):
            other[i, :, 0:BLK] = other_parts[i, 0]
            other[i, :, BLK:WIDE] = jnp.where(half[0:PAD], other_parts[i, 2], other_parts[i, 1])
        pl.when(z == 6)(to_fifth.start)
        pl.when(z == 11)(to_zero.start)

    @pl.when(z == 11)
    def _():
        to_below.start()

    to_above.wait_recv()

    @pl.when(jnp.logical_not(last))
    def _():
        to_below.start()

    ext_lane = lax.broadcasted_iota(jnp.int32, (8, WIDE), 1)
    block = jnp.where(ext_lane < BLK, h, jnp.where(ext_lane < BLK + BLK // 2, h + 1, h - 1)).astype(jnp.float32)
    up_ok = jnp.where(m > 0, 1.0, 0.0)
    down_ok = jnp.where(m < SLABS - 1, 1.0, 0.0)
    all_copy = pltpu.make_async_remote_copy(
        par, par, all_send, all_recv, across(0, 0), MESH
    )

    def neighbours(ref, at, size):
        mid = ref[pl.ds(at, size)]
        return (ref[pl.ds(at - 1, size)] + ref[pl.ds(at + 1, size)]) + (
            pltpu.roll(mid, 1, 2) + pltpu.roll(mid, WIDE - 1, 2)
        )

    def lift(rows):
        for r in rows:
            cur_b[r] = jnp.broadcast_to(field[0, r : r + 1, :], (8, WIDE))
            con_b[r] = jnp.broadcast_to(field[1, r : r + 1, :], (8, WIDE))

    def sweeps(g, spans_a, spans_b, spans_q):
        numbers = par[pl.ds(pl.multiple_of(g * 8, 8), 8), :]
        om = jnp.broadcast_to(BASE_FREQ * numbers[:, 0:1], (8, WIDE))
        am = jnp.broadcast_to(numbers[:, 1:2], (8, WIDE))
        ct = jnp.broadcast_to(numbers[:, 2:3], (8, WIDE))
        mask = jnp.where(jnp.logical_and(block >= 0.0, block < ct), 1.0, 0.0)
        scale = 0.5 * (om * om) * (am * am) * mask

        def first_sweep(at, size, ok):
            con, cur = con_b[pl.ds(at, size)], cur_b[pl.ds(at, size)]
            product = om[None] * con
            inverse = 1.0 / (16.0 + product * product)
            masked = inverse * (mask * ok)[None]
            re = 4.0 * masked
            im = -(product * masked)
            inv_r[pl.ds(at, size)] = re
            inv_i[pl.ds(at, size)] = im
            a_r[pl.ds(at, size)] = cur * re
            a_i[pl.ds(at, size)] = cur * im
            weight[pl.ds(at, size)] = (scale[None] * con) * inverse

        def second_sweep(at, size):
            near_r = cur_b[pl.ds(at, size)] + neighbours(a_r, at, size)
            near_i = neighbours(a_i, at, size)
            re, im = inv_r[pl.ds(at, size)], inv_i[pl.ds(at, size)]
            b_r[pl.ds(at, size)] = near_r * re - near_i * im
            b_i[pl.ds(at, size)] = near_r * im + near_i * re

        def third_sweep(at, size):
            near_r = cur_b[pl.ds(at, size)] + neighbours(b_r, at, size)
            near_i = neighbours(b_i, at, size)
            loss = weight[pl.ds(at, size)] * (near_r * near_r + near_i * near_i)
            total[pl.ds(at, size)] = total[pl.ds(at, size)] + loss

        for span in spans_a:
            first_sweep(*span)
        for span in spans_b:
            second_sweep(*span)
        for span in spans_q:
            third_sweep(*span)

    end = PAD + ROWS

    def middle(g):
        sweeps(
            g,
            [(at, 4, 1.0) for at in range(PAD, end, 4)],
            [(at, 3) for at in range(PAD + 1, end - 1, 3)],
            [(at, 4) for at in range(PAD + 2, end - 2, 4)],
        )

    def rims(g):
        sweeps(
            g,
            [(3, 3, up_ok), (6, 2, up_ok), (8, 4, 1.0), (end - 4, 4, 1.0), (end, 2, down_ok), (end + 2, 3, down_ok)],
            [(4, 4), (8, 3), (end - 3, 4), (end + 1, 3)],
            [(5, 5), (end - 2, 5)],
        )

    def rows_of(g):
        def rows_here(at, size):
            rows = par.at[pl.ds(at, size)]
            pltpu.make_async_remote_copy(rows, rows, send_sem, recv_sem.at[g], below, MESH).wait_recv()

        @pl.when(low)
        def _():
            @pl.when(g == 0)
            def _():
                rows_here(1, 7)

            pl.when(g > 0)(lambda: rows_here(0, 8))

        @pl.when(jnp.logical_and(low, g == 3))
        def _():
            all_copy.start()

        @pl.when(jnp.logical_and(high, g == 0))
        def _():
            all_copy.wait_recv()


    def early(g, t):
        rows_of(g)
        middle(g)
        return t

    def early_rims(g, t):
        rims(g)
        return t

    def late(g, t):
        rows_of(g)
        middle(g)
        rims(g)
        return t

    def start_total(i, t):
        total[pl.ds(4 + 4 * i, 4)] = jnp.zeros((4, 8, WIDE), jnp.float32)
        return t

    lax.fori_loop(0, 10, start_total, 0)
    lift(range(PAD, end))

    ahead = jnp.where(low, 2, 0)
    lax.fori_loop(0, ahead, early, 0)

    to_below.wait_recv()

    @pl.when(z == 6)
    def _():
        to_above.start()

    lift([*range(3, PAD), *range(end, end + 5)])
    lax.fori_loop(0, ahead, early_rims, 0)
    lax.fori_loop(ahead, 4, late, 0)

    packed[...] = jnp.zeros_like(packed)
    for r in range(5, TALL - 5):
        packed[r : r + 1, :] = jnp.sum(total[r], axis=0, keepdims=True)
    row = lax.broadcasted_iota(jnp.int32, (TALL, WIDE), 0)
    col = lax.broadcasted_iota(jnp.int32, (TALL, WIDE), 1)
    in_grid = jnp.logical_and(
        jnp.logical_and(jnp.logical_or(row >= PAD, m > 0), jnp.logical_or(row < PAD + ROWS, m < SLABS - 1)),
        jnp.logical_and(
            jnp.logical_or(col < BLK + BLK // 2, h > 0),
            jnp.logical_or(jnp.logical_or(col < BLK, col >= BLK + BLK // 2), h < HARMS - 1),
        ),
    )
    share = jnp.where(in_grid, 1.0 / (4.0 + field[2]), 0.0)
    mean = packed[...]
    warm = mean * share
    for sweep in range(3):
        warm = (
            mean
            + (pltpu.roll(warm, 1, 0) + pltpu.roll(warm, TALL - 1, 0))
            + (pltpu.roll(warm, 1, 1) + pltpu.roll(warm, WIDE - 1, 1))
        ) * share
    both[0] = mean[PAD : PAD + ROWS, 0:BLK]
    both[1] = warm[PAD : PAD + ROWS, 0:BLK]

    def rows_sent(size):
        rows = par.at[pl.ds(0, size)]
        pltpu.make_async_remote_copy(rows, rows, send_sem, recv_sem.at[0], below, MESH).wait_send()

    @pl.when(z != 5)
    def _():
        to_below.wait_send()

    @pl.when(z == 11)
    def _():
        to_zero.wait_send()


    @pl.when(z != 0)
    def _():
        to_above.wait_send()

    @pl.when(z == 6)
    def _():
        to_fifth.wait_send()

    @pl.when(high)
    def _():
        rows_sent(RING)

    @pl.when(low)
    def _():
        all_copy.wait_send()
        rows_sent(RING - 1)


def exchange_and_solve(current_pattern, conductivity, cooling, harm_order, harm_amp, block_counts):
    f32 = jnp.float32
    tall = pltpu.VMEM((TALL, 8, WIDE), f32)
    return pl.pallas_call(
        kernel,
        out_shape=jax.ShapeDtypeStruct((2, ROWS, BLK), f32),
        in_specs=[pl.BlockSpec(memory_space=pltpu.HBM)] * 3 + [pl.BlockSpec(memory_space=pltpu.SMEM)] * 3,
        out_specs=pl.BlockSpec(memory_space=pltpu.VMEM),
        scratch_shapes=[
            pltpu.VMEM((3, TALL, WIDE), f32),
            pltpu.VMEM((3, 3, ROWS, BLK), f32),
            pltpu.VMEM((3, PAD, WIDE), f32),
            pltpu.VMEM((3, 3, PAD, BLK), f32),
            pltpu.VMEM((1, BLK), f32),
            pltpu.VMEM((HARMS, BLK), f32),
            tall, tall, tall, tall, tall, tall, tall, tall, tall, tall,
            pltpu.VMEM((TALL, WIDE), f32),
            pltpu.SemaphoreType.DMA,
            pltpu.SemaphoreType.DMA,
            pltpu.SemaphoreType.DMA,
            pltpu.SemaphoreType.DMA((4,)),
            pltpu.SemaphoreType.DMA((3,)),
            pltpu.SemaphoreType.DMA((2,)),
            pltpu.SemaphoreType.DMA,
            pltpu.SemaphoreType.DMA,
        ],
        compiler_params=pltpu.CompilerParams(collective_id=0, has_side_effects=True),
    )(current_pattern, conductivity, cooling, harm_order, harm_amp, block_counts)


def on_device(*args):
    both = lax.cond(
        lax.axis_index("harm") < HARMS,
        exchange_and_solve,
        lambda *a: jnp.zeros((2, ROWS, BLK), jnp.float32),
        *args,
    )
    return both[0] * (1.0 / HARMS), both[1] * (1.0 / HARMS)


def solution(mesh):
    return jax.shard_map(
        on_device,
        mesh=mesh,
        in_specs=(
            P("mesh", None),
            P("mesh", None),
            P("mesh", None),
            P("harm"),
            P("harm"),
            P("harm"),
        ),
        out_specs=(P("mesh", "harm"), P("mesh", "harm")),
        check_vma=False,
    )
```

time: 28.7 us -> 27.1 us (0.944)
  Pallas kernels: 27.2 us -> 25.6 us
    pallas_call x1, Pallas kernels: 27.2 us -> 25.6 us  [exchange_and_solve(): pl.pallas_call(kernel, out_shape=jax.ShapeDtypeStruct((2, ROWS, BLK), f32...]
where the time goes in v3:
time: 27.1 us; the launch traced here: 26.8 us
  Pallas kernels  25.6 us (94%)
  between operations  0.64 us (2%)
  other arithmetic  0.62 us (2%)
    pallas_call x1, Pallas kernels, exchange_and_solve(): pl.pallas_call(kernel, out_shape=jax.ShapeDtypeStruct((2, ROWS, BLK), f32...  25.6 us
    mul x1, other arithmetic, on_device(): return (both[0] * (1.0 / HARMS), both[1] * (1.0 / HARMS))  0.62 us

profile of v3, /device:TPU:1, one launch (start us, length us, event | category | flops | bytes accessed | tf_op | source)
XLA Modules:
  0.0 26.8 jit_solution(3170469004716341250)
XLA Ops:
  0.6 25.6 %conditional.1 = (f32[2,32,128]{2,1,0:T(8,128)S(1)}) conditional(s32[]{:T(128)} %convert_element_type.3, () %tuple.14, (f32[32,4096]{1,0:T(8,128)}, f32[32,4096]{1,0:T(8,128)}, f32[32,4096]{1,0:T(8,128)}, s32[1]{0:T(128)}, s32[1]{0:T(128)}, /*index=5*/s32[1]{0:T(128)}) %tuple.15), branch_computations={%region_0.0_spmd, %region_1.0_spmd} | conditional | bytes 32780 | solution.py:401
  0.6 25.6 %branch_1_fun.1 = f32[2,32,128]{2,1,0:T(8,128)S(1)} custom-call(f32[32,4096]{1,0:T(8,128)} %get-tuple-element.29.current, f32[32,4096]{1,0:T(8,128)} %get-tuple-element.30.conductivity, f32[32,4096]{1,0:T(8,128)} %get-tuple-element.31.cooling, s32[1]{0:T(128)} %get-tuple-element.32.order, s32[1]{0:T(128)} %get-tuple-element.33.amp, s32[1]{0:T(128)} %get-tuple-element.34.count), custom_call_target="tpu_custom_call" | custom-call | tf_op jit(solution)/shard_map/cond/branch_1_fun/pallas_call | solution.py:373
  26.2 0.6 %multiply_bitcast_fusion = (f32[32,128]{1,0:T(8,128)}, f32[32,128]{1,0:T(8,128)}) fusion(f32[2,32,128]{2,1,0:T(8,128)S(1)} %get-tuple-element.37), kind=kLoop, calls=%fused_computation | loop fusion | flops 8192 | bytes 65536 | tf_op jit(solution)/shard_map/mul | solution.py:407

commit v4 on v3

--- a/solution.py
+++ b/solution.py
@@ -28,7 +28,7 @@
 
 def kernel(
     current, conductivity, cooling, order, amp, count, both,
-    field, parts, other, other_parts, msg, par, cur_b, con_b, inv_r, inv_i, a_r, a_i, b_r, b_i, weight, total, packed,
+    field, parts, other, other_parts, msg, par, cur_b, con_b, inv_r, inv_i, a_r, a_i, b_r, b_i, weight, total, packed, rec,
     load_sem, other_sem, send_sem, recv_sem, edge_send, edge_recv, all_send, all_recv,
 ):
     m, h = lax.axis_index("mesh"), lax.axis_index("harm")
@@ -46,7 +46,9 @@
     own_half = [2 * z_hi + c, 2 * z_hi + (1 - c)]
     other_half = [2 * (1 - z_hi) + c, 2 * (1 - z_hi) + (1 - c)]
     around_y = [4 * jnp.where(y + d >= 8, y + d - 8, y + d) for d in range(8)]
-    mirror = jnp.where(z_lo < 3, m + 3, m - 3)
+    low_move = jnp.where(z_lo == 0, 4, jnp.where(z_lo == 1, 2, jnp.where(z_lo == 2, 3, -3)))
+    high_move = jnp.where(z_lo == 4, -4, jnp.where(z_lo == 3, -2, jnp.where(z_lo == 5, -3, 3)))
+    mirror = m + jnp.where(low, low_move, high_move)
 
     def inside(dy, dc):
         return m, around_y[dy % 8] + own_half[dc]
@@ -117,30 +119,7 @@
             MESH,
         )
 
-    @pl.when(high)
-    def _():
-        for i in range(RING):
-            row_copy(i, 1).start()
-
-    @pl.when(low)
-    def _():
-        par[0:1, :] = msg[...]
-        for i in range(RING - 1):
-            row_copy(i, 0).start()
-
-    pltpu.make_async_copy(parts, parts, load_sem).wait()
     half = lax.broadcasted_iota(jnp.int32, (ROWS, BLK), 1) < BLK // 2
-    for i in range(3):
-        field[i, PAD : PAD + ROWS, 0:BLK] = parts[i, 0]
-        field[i, PAD : PAD + ROWS, BLK:WIDE] = jnp.where(half, parts[i, 2], parts[i, 1])
-
-    to_below = pltpu.make_async_remote_copy(
-        field.at[:, pl.ds(ROWS, PAD)], field.at[:, pl.ds(0, PAD)], edge_send.at[0], edge_recv.at[0], below, MESH
-    )
-    to_above = pltpu.make_async_remote_copy(
-        field.at[:, pl.ds(PAD, PAD)], field.at[:, pl.ds(PAD + ROWS, PAD)], edge_send.at[1], edge_recv.at[1], above, MESH
-    )
-
     to_fifth = pltpu.make_async_remote_copy(
         other,
         field.at[:, pl.ds(PAD + ROWS, PAD)],
@@ -154,10 +133,6 @@
         other, field.at[:, pl.ds(0, PAD)], edge_send.at[2], edge_recv.at[0], (after, h - 2), MESH
     )
 
-    @pl.when(z_lo != 0)
-    def _():
-        to_above.start()
-
     @pl.when(lends)
     def _():
         pltpu.make_async_copy(other_parts, other_parts, other_sem).wait()
@@ -166,6 +141,33 @@
             other[i, :, BLK:WIDE] = jnp.where(half[0:PAD], other_parts[i, 2], other_parts[i, 1])
         pl.when(z == 6)(to_fifth.start)
         pl.when(z == 11)(to_zero.start)
+
+    @pl.when(high)
+    def _():
+        for i in range(RING):
+            row_copy(i, 1).start()
+
+    @pl.when(low)
+    def _():
+        par[0:1, :] = msg[...]
+        for i in range(RING - 1):
+            row_copy(i, 0).start()
+
+    pltpu.make_async_copy(parts, parts, load_sem).wait()
+    for i in range(3):
+        field[i, PAD : PAD + ROWS, 0:BLK] = parts[i, 0]
+        field[i, PAD : PAD + ROWS, BLK:WIDE] = jnp.where(half, parts[i, 2], parts[i, 1])
+
+    to_below = pltpu.make_async_remote_copy(
+        field.at[:, pl.ds(ROWS, PAD)], field.at[:, pl.ds(0, PAD)], edge_send.at[0], edge_recv.at[0], below, MESH
+    )
+    to_above = pltpu.make_async_remote_copy(
+        field.at[:, pl.ds(PAD, PAD)], field.at[:, pl.ds(PAD + ROWS, PAD)], edge_send.at[1], edge_recv.at[1], above, MESH
+    )
+
+    @pl.when(z_lo != 0)
+    def _():
+        to_above.start()
 
     @pl.when(z == 11)
     def _():
@@ -208,9 +210,8 @@
             con, cur = con_b[pl.ds(at, size)], cur_b[pl.ds(at, size)]
             product = om[None] * con
             inverse = 1.0 / (16.0 + product * product)
-            masked = inverse * (mask * ok)[None]
-            re = 4.0 * masked
-            im = -(product * masked)
+            re = inverse * (mask * (4.0 * ok))[None]
+            im = product * (inverse * (mask * -ok)[None])
             inv_r[pl.ds(at, size)] = re
             inv_i[pl.ds(at, size)] = im
             a_r[pl.ds(at, size)] = cur * re
@@ -308,13 +309,6 @@
     def _():
         to_above.start()
 
-    lift([*range(3, PAD), *range(end, end + 5)])
-    lax.fori_loop(0, ahead, early_rims, 0)
-    lax.fori_loop(ahead, 4, late, 0)
-
-    packed[...] = jnp.zeros_like(packed)
-    for r in range(5, TALL - 5):
-        packed[r : r + 1, :] = jnp.sum(total[r], axis=0, keepdims=True)
     row = lax.broadcasted_iota(jnp.int32, (TALL, WIDE), 0)
     col = lax.broadcasted_iota(jnp.int32, (TALL, WIDE), 1)
     in_grid = jnp.logical_and(
@@ -324,7 +318,15 @@
             jnp.logical_or(jnp.logical_or(col < BLK, col >= BLK + BLK // 2), h < HARMS - 1),
         ),
     )
-    share = jnp.where(in_grid, 1.0 / (4.0 + field[2]), 0.0)
+    rec[...] = jnp.where(in_grid, 1.0 / (4.0 + field[2]), 0.0)
+    packed[...] = jnp.zeros_like(packed)
+    lift([*range(3, PAD), *range(end, end + 5)])
+    lax.fori_loop(0, ahead, early_rims, 0)
+    lax.fori_loop(ahead, 4, late, 0)
+
+    for r in range(5, TALL - 5):
+        packed[r : r + 1, :] = jnp.sum(total[r], axis=0, keepdims=True)
+    share = rec[...]
     mean = packed[...]
     warm = mean * share
     for sweep in range(3):
@@ -384,6 +386,7 @@
             pltpu.VMEM((HARMS, BLK), f32),
             tall, tall, tall, tall, tall, tall, tall, tall, tall, tall,
             pltpu.VMEM((TALL, WIDE), f32),
+            pltpu.VMEM((TALL, WIDE), f32),
             pltpu.SemaphoreType.DMA,
             pltpu.SemaphoreType.DMA,
             pltpu.SemaphoreType.DMA,

time: 27.1 us -> 26.5 us (0.978)
  Pallas kernels: 25.6 us -> 25 us
    pallas_call x1, Pallas kernels: 25.6 us -> 25 us  [exchange_and_solve(): pl.pallas_call(kernel, out_shape=jax.ShapeDtypeStruct((2, ROWS, BLK), f32...]
where the time goes in v4:
time: 26.5 us; the launch traced here: 26.3 us
  Pallas kernels  25 us (94%)
  between operations  0.64 us (2%)
  other arithmetic  0.62 us (2%)
    pallas_call x1, Pallas kernels, exchange_and_solve(): pl.pallas_call(kernel, out_shape=jax.ShapeDtypeStruct((2, ROWS, BLK), f32...  25 us
    mul x1, other arithmetic, on_device(): return (both[0] * (1.0 / HARMS), both[1] * (1.0 / HARMS))  0.62 us

profile of v4, /device:TPU:1, one launch (start us, length us, event | category | flops | bytes accessed | tf_op | source)
XLA Modules:
  0.0 26.3 jit_solution(17786967730166370167)
XLA Ops:
  0.6 25.1 %conditional.1 = (f32[2,32,128]{2,1,0:T(8,128)S(1)}) conditional(s32[]{:T(128)} %convert_element_type.3, () %tuple.14, (f32[32,4096]{1,0:T(8,128)}, f32[32,4096]{1,0:T(8,128)}, f32[32,4096]{1,0:T(8,128)}, s32[1]{0:T(128)}, s32[1]{0:T(128)}, /*index=5*/s32[1]{0:T(128)}) %tuple.15), branch_computations={%region_0.0_spmd, %region_1.0_spmd} | conditional | bytes 32780 | solution.py:404
  0.6 25.0 %branch_1_fun.1 = f32[2,32,128]{2,1,0:T(8,128)S(1)} custom-call(f32[32,4096]{1,0:T(8,128)} %get-tuple-element.29.current, f32[32,4096]{1,0:T(8,128)} %get-tuple-element.30.conductivity, f32[32,4096]{1,0:T(8,128)} %get-tuple-element.31.cooling, s32[1]{0:T(128)} %get-tuple-element.32.order, s32[1]{0:T(128)} %get-tuple-element.33.amp, s32[1]{0:T(128)} %get-tuple-element.34.count), custom_call_target="tpu_custom_call" | custom-call | tf_op jit(solution)/shard_map/cond/branch_1_fun/pallas_call | solution.py:375
  25.7 0.6 %multiply_bitcast_fusion = (f32[32,128]{1,0:T(8,128)}, f32[32,128]{1,0:T(8,128)}) fusion(f32[2,32,128]{2,1,0:T(8,128)S(1)} %get-tuple-element.37), kind=kLoop, calls=%fused_computation | loop fusion | flops 8192 | bytes 65536 | tf_op jit(solution)/shard_map/mul | solution.py:410

commit v5 on v4

--- a/solution.py
+++ b/solution.py
@@ -58,6 +58,32 @@
 
     barrier = pltpu.get_barrier_semaphore()
 
+    def greet(who):
+        pl.semaphore_signal(barrier, inc=1, device_id=who, device_id_type=MESH)
+
+    @pl.when(jnp.logical_not(last))
+    def _():
+        greet(below)
+
+    @pl.when(z == 5)
+    def _():
+        greet((after, h + 2))
+
+    @pl.when(z == 6)
+    def _():
+        greet(above)
+
+    @pl.when(z == 0)
+    def _():
+        greet((before, h + 2))
+
+    @pl.when(low)
+    def _():
+        for dy, dc in AROUND[:-1]:
+            greet(inside(dy, dc))
+        for dy, dc in AROUND:
+            greet(across(dy, dc))
+
     left = jnp.maximum(h - 1, 0)
     right = jnp.minimum(h + 1, HARMS - 1)
     for i, source in enumerate((current, conductivity, cooling)):
@@ -73,32 +99,6 @@
             for j, block in enumerate((h - 2, jnp.maximum(h - 3, 0), h - 1)):
                 columns = pl.ds(pl.multiple_of(block * BLK, BLK), BLK)
                 pltpu.make_async_copy(source.at[lent_rows, columns], other_parts.at[i, j], other_sem).start()
-
-    def greet(who):
-        pl.semaphore_signal(barrier, inc=1, device_id=who, device_id_type=MESH)
-
-    @pl.when(jnp.logical_not(last))
-    def _():
-        greet(below)
-
-    @pl.when(z == 5)
-    def _():
-        greet((after, h + 2))
-
-    @pl.when(z == 6)
-    def _():
-        greet(above)
-
-    @pl.when(z == 0)
-    def _():
-        greet((before, h + 2))
-
-    @pl.when(low)
-    def _():
-        for dy, dc in AROUND[:-1]:
-            greet(inside(dy, dc))
-        for dy, dc in AROUND:
-            greet(across(dy, dc))
 
     lane = lax.broadcasted_iota(jnp.int32, (1, BLK), 1)
     numbers = [jnp.full((1, BLK), v[0], jnp.int32) for v in (order, amp, count)]
@@ -133,6 +133,17 @@
         other, field.at[:, pl.ds(0, PAD)], edge_send.at[2], edge_recv.at[0], (after, h - 2), MESH
     )
 
+    @pl.when(high)
+    def _():
+        for i in range(RING):
+            row_copy(i, 1).start()
+
+    @pl.when(low)
+    def _():
+        par[0:1, :] = msg[...]
+        for i in range(RING - 1):
+            row_copy(i, 0).start()
+
     @pl.when(lends)
     def _():
         pltpu.make_async_copy(other_parts, other_parts, other_sem).wait()
@@ -141,17 +152,6 @@
             other[i, :, BLK:WIDE] = jnp.where(half[0:PAD], other_parts[i, 2], other_parts[i, 1])
         pl.when(z == 6)(to_fifth.start)
         pl.when(z == 11)(to_zero.start)
-
-    @pl.when(high)
-    def _():
-        for i in range(RING):
-            row_copy(i, 1).start()
-
-    @pl.when(low)
-    def _():
-        par[0:1, :] = msg[...]
-        for i in range(RING - 1):
-            row_copy(i, 0).start()
 
     pltpu.make_async_copy(parts, parts, load_sem).wait()
     for i in range(3):

time: 26.5 us -> 26.5 us (level)
  no operation moved by 1% of the time
where the time goes in v5:
time: 26.5 us; the launch traced here: 26.3 us
  Pallas kernels  25 us (94%)
  between operations  0.64 us (2%)
  other arithmetic  0.62 us (2%)
    pallas_call x1, Pallas kernels, exchange_and_solve(): pl.pallas_call(kernel, out_shape=jax.ShapeDtypeStruct((2, ROWS, BLK), f32...  25 us
    mul x1, other arithmetic, on_device(): return (both[0] * (1.0 / HARMS), both[1] * (1.0 / HARMS))  0.62 us

profile of v5, /device:TPU:1, one launch (start us, length us, event | category | flops | bytes accessed | tf_op | source)
XLA Modules:
  0.0 26.3 jit_solution(6112785923082319695)
XLA Ops:
  0.6 25.0 %conditional.1 = (f32[2,32,128]{2,1,0:T(8,128)S(1)}) conditional(s32[]{:T(128)} %convert_element_type.3, () %tuple.14, (f32[32,4096]{1,0:T(8,128)}, f32[32,4096]{1,0:T(8,128)}, f32[32,4096]{1,0:T(8,128)}, s32[1]{0:T(128)}, s32[1]{0:T(128)}, /*index=5*/s32[1]{0:T(128)}) %tuple.15), branch_computations={%region_0.0_spmd, %region_1.0_spmd} | conditional | bytes 32780 | solution.py:404
  0.6 25.0 %branch_1_fun.1 = f32[2,32,128]{2,1,0:T(8,128)S(1)} custom-call(f32[32,4096]{1,0:T(8,128)} %get-tuple-element.29.current, f32[32,4096]{1,0:T(8,128)} %get-tuple-element.30.conductivity, f32[32,4096]{1,0:T(8,128)} %get-tuple-element.31.cooling, s32[1]{0:T(128)} %get-tuple-element.32.order, s32[1]{0:T(128)} %get-tuple-element.33.amp, s32[1]{0:T(128)} %get-tuple-element.34.count), custom_call_target="tpu_custom_call" | custom-call | tf_op jit(solution)/shard_map/cond/branch_1_fun/pallas_call | solution.py:375
  25.7 0.6 %multiply_bitcast_fusion = (f32[32,128]{1,0:T(8,128)}, f32[32,128]{1,0:T(8,128)}) fusion(f32[2,32,128]{2,1,0:T(8,128)S(1)} %get-tuple-element.37), kind=kLoop, calls=%fused_computation | loop fusion | flops 8192 | bytes 65536 | tf_op jit(solution)/shard_map/mul | solution.py:410
